TPU v7x, 32 devices: a whole 2x2x4 slice. The times are simulated.
32 devices in a mesh: freq: 2 (over y), tile: 8 (over z, x), src: 2 (over core).
Axes of the slice: x: 2, y: 2, z: 4, core: 2. Of those that a mesh axis runs over, the one named last changes fastest.
Arguments:
- green: bfloat16 [2, 4096, 1024], P(None, ('freq', 'tile'), 'src'), parts along dimension 1, may hold values from -0.1875 to 0.1875
- direction: bfloat16 [2, 2048, 1024], P(None, ('freq', 'src')), parts along dimension 1, may hold values from -6 to 6
- partners: int32 [32, 8], P(('freq', 'tile')), parts along dimension 0, may hold values from 0 to 15, as said below
- counts: int32 [32], P(('freq', 'tile')), parts along dimension 0, may hold values from 1 to 8, as said below
Outputs:
- hessian: float32 [2048, 2, 1024], P(('freq', 'tile'), None, 'src'), parts along dimension 0
There are 2 independent parts, one for each index of `freq`. A program takes and returns all parts, laid end to end along the dimension named above; each array names one. Nothing has to cross between parts.
Inputs may be any that keep to these rules, and one draw needn't show every extreme that they name: The entries partners[t, k] of a row are distinct tile indices u with |u // 2 - t // 2| <= 3; only those with k < counts[t] are sampled. `counts`: some tile row has all 8 slots sampled, and some tile row has only one.
All inputs are finite; a program needn't handle non-finite values.
Results may differ from a plain program's by a relative error of at most 0.0016.
Values may be sent and summed in bfloat16 or wider, within the bound.
A program may use at most 64 MiB of HBM per device.

v0:
```python
import jax
import jax.numpy as jnp
from jax import lax
from jax.sharding import PartitionSpec as P

BAND_DEV = 3


def from_behind(value, axis, steps):
    count = lax.axis_size(axis)
    first, last = (max(0, -steps), min(count, count - steps))
    return lax.ppermute(value, axis, [(source, source + steps) for source in range(first, last)])


def shards(green, direction, partners, counts):
    tile_dev, kmax = partners.shape
    rows = green.shape[1]
    half = green.shape[2]
    tile = rows // tile_dev
    real_part = jnp.dot(green[0], direction[0], preferred_element_type=jnp.float32) - jnp.dot(
        green[1], direction[1], preferred_element_type=jnp.float32
    )
    imag_part = jnp.dot(green[0], direction[1], preferred_element_type=jnp.float32) + jnp.dot(
        green[1], direction[0], preferred_element_type=jnp.float32
    )
    images = lax.psum_scatter(
        jnp.stack([real_part, imag_part]), "src", scatter_dimension=2, tiled=True
    ).astype(jnp.bfloat16)
    tiles = green.reshape(2, tile_dev, tile, half)
    count_tile = lax.axis_size("tile")
    reach = min(BAND_DEV, count_tile - 1)
    empty = jnp.zeros_like(tiles)
    offsets = [offset for offset in range(-reach, reach + 1) if offset != 0]
    moved = [from_behind(tiles, "tile", -offset) for offset in offsets]
    nearby = dict(zip(offsets, moved))
    nearby[0] = tiles
    window = jnp.concatenate(
        [nearby.get(offset, empty) for offset in range(-BAND_DEV, BAND_DEV + 1)], axis=1
    )
    first_tile = (lax.axis_index("tile") - BAND_DEV) * tile_dev
    local_index = partners - first_tile
    live = (jnp.arange(kmax, dtype=jnp.int32)[None, :] < counts[:, None]).astype(jnp.float32)
    across = (((1,), (1,)), ((), ()))
    stacks = []
    pieces = []
    for row in range(tile_dev):
        stack = jnp.take(window, local_index[row], axis=1).reshape(2, kmax * tile, half)
        stacks.append(stack)
        image_row = images[:, row * tile : (row + 1) * tile]
        couple_real = lax.dot_general(
            image_row[0], stack[0], across, preferred_element_type=jnp.float32
        ) + lax.dot_general(image_row[1], stack[1], across, preferred_element_type=jnp.float32)
        couple_imag = lax.dot_general(
            image_row[1], stack[0], across, preferred_element_type=jnp.float32
        ) - lax.dot_general(image_row[0], stack[1], across, preferred_element_type=jnp.float32)
        blocks = jnp.stack([couple_real, couple_imag]).reshape(2, tile, kmax, tile)
        pieces.append(blocks * live[row][None, None, :, None])
    partial_blocks = jnp.stack(pieces, axis=1)
    coupling = lax.psum(partial_blocks, "src").astype(jnp.bfloat16)
    weight_rows = []
    for row in range(tile_dev):
        stack = stacks[row]
        flat = coupling[:, row].reshape(2, tile, kmax * tile)
        weight_real = jnp.dot(flat[0], stack[0], preferred_element_type=jnp.float32) - jnp.dot(
            flat[1], stack[1], preferred_element_type=jnp.float32
        )
        weight_imag = jnp.dot(flat[0], stack[1], preferred_element_type=jnp.float32) + jnp.dot(
            flat[1], stack[0], preferred_element_type=jnp.float32
        )
        weight_rows.append(jnp.stack([weight_real, weight_imag]))
    weighted = jnp.concatenate(weight_rows, axis=1).astype(jnp.bfloat16)
    full_rows = lax.all_gather(green, "src", axis=2, tiled=True)
    down = (((0,), (0,)), ((), ()))
    out_real = lax.dot_general(
        full_rows[0], weighted[0], down, preferred_element_type=jnp.float32
    ) + lax.dot_general(full_rows[1], weighted[1], down, preferred_element_type=jnp.float32)
    out_imag = lax.dot_general(
        full_rows[0], weighted[1], down, preferred_element_type=jnp.float32
    ) - lax.dot_general(full_rows[1], weighted[0], down, preferred_element_type=jnp.float32)
    return lax.psum_scatter(
        jnp.stack([out_real, out_imag], axis=1), "tile", scatter_dimension=0, tiled=True
    )


def solution(mesh):
    in_specs = (
        P(None, ("freq", "tile"), "src"),
        P(None, ("freq", "src"), None),
        P(("freq", "tile"), None),
        P(("freq", "tile")),
    )
    out_specs = P(("freq", "tile"), None, "src")
    return jax.shard_map(shards, mesh=mesh, in_specs=in_specs, out_specs=out_specs, check_vma=False)
```

profile of v0, /device:TPU:0, one launch (start us, length us, event | category | flops | bytes accessed | tf_op | source)
XLA Modules:
  0.0 209.8 jit_solution(5152656841434377165)
XLA Ops:
  6.5 1.9 fusion.14
  8.5 1.4 fusion.18
  10.8 1.5 pad_maximum_fusion.1
  12.4 6.8 %collective-permute-start = (bf16[2,2,128,512]{3,2,1,0:T(8,128)(2,1)S(1)}, bf16[2,2,128,512]{3,2,1,0:T(8,128)(2,1)}, u32[]{:S(2)}, u32[]{:S(2)}) collective-permute-start(bf16[2,2,128,512]{3,2,1,0:T(8,128)(2,1)S(1)} %bitcast.167), channel_id=1, source_target_pairs={{0,6},{2,8},{4,10},{6,12},{8,14},{1,7},{3,9},{5,11},{7,13},{9,15},... | collective-permute-start | bytes 1572872 | tf_op jit(solution)/shard_map/ppermute | solution.py:12
  19.2 3.5 %collective-permute-start.1 = (bf16[2,2,128,512]{3,2,1,0:T(8,128)(2,1)S(1)}, bf16[2,2,128,512]{3,2,1,0:T(8,128)(2,1)S(1)}, u32[]{:S(2)}, u32[]{:S(2)}) collective-permute-start(bf16[2,2,128,512]{3,2,1,0:T(8,128)(2,1)S(1)} %bitcast.168), channel_id=1, source_target_pairs={{0,4},{2,6},{4,8},{6,10},{8,12},{10,14},{1,5},{3,7},{5,9},{7,11},{... | collective-permute-start | bytes 1572872 | tf_op jit(solution)/shard_map/ppermute | solution.py:12
  22.7 2.7 %collective-permute-start.2 = (bf16[2,2,128,512]{3,2,1,0:T(8,128)(2,1)S(1)}, bf16[2,2,128,512]{3,2,1,0:T(8,128)(2,1)S(1)}, u32[]{:S(2)}, u32[]{:S(2)}) collective-permute-start(bf16[2,2,128,512]{3,2,1,0:T(8,128)(2,1)S(1)} %bitcast.169), channel_id=1, source_target_pairs={{0,2},{2,4},{4,6},{6,8},{8,10},{10,12},{12,14},{1,3},{3,5},{5,7},{... | collective-permute-start | bytes 1572872 | tf_op jit(solution)/shard_map/ppermute | solution.py:12
  25.4 1.3 collective-permute-start.3
  28.3 2.5 %collective-permute-done = bf16[2,2,128,512]{3,2,1,0:T(8,128)(2,1)} collective-permute-done((bf16[2,2,128,512]{3,2,1,0:T(8,128)(2,1)S(1)}, bf16[2,2,128,512]{3,2,1,0:T(8,128)(2,1)}, u32[]{:S(2)}, u32[]{:S(2)}) %collective-permute-start) | collective-permute-done | bytes 524320 | tf_op jit(solution)/shard_map/ppermute | solution.py:12
  32.0 1.9 constant_dynamic-update-slice_fusion.6
  33.9 6.9 %collective-permute-done.1 = bf16[2,2,128,512]{3,2,1,0:T(8,128)(2,1)S(1)} collective-permute-done((bf16[2,2,128,512]{3,2,1,0:T(8,128)(2,1)S(1)}, bf16[2,2,128,512]{3,2,1,0:T(8,128)(2,1)S(1)}, u32[]{:S(2)}, u32[]{:S(2)}) %collective-permute-start.1) | collective-permute-done | bytes 524320 | tf_op jit(solution)/shard_map/ppermute | solution.py:12
  41.7 5.6 %collective-permute-done.2 = bf16[2,2,128,512]{3,2,1,0:T(8,128)(2,1)S(1)} collective-permute-done((bf16[2,2,128,512]{3,2,1,0:T(8,128)(2,1)S(1)}, bf16[2,2,128,512]{3,2,1,0:T(8,128)(2,1)S(1)}, u32[]{:S(2)}, u32[]{:S(2)}) %collective-permute-start.2) | collective-permute-done | bytes 524320 | tf_op jit(solution)/shard_map/ppermute | solution.py:12
  49.8 2.5 %collective-permute-done.4 = bf16[2,2,128,512]{3,2,1,0:T(8,128)(2,1)S(1)} collective-permute-done((bf16[2,2,128,512]{3,2,1,0:T(8,128)(2,1)S(1)}, bf16[2,2,128,512]{3,2,1,0:T(8,128)(2,1)S(1)}, u32[]{:S(2)}, u32[]{:S(2)}) %collective-permute-start.4) | collective-permute-done | bytes 524320 | tf_op jit(solution)/shard_map/ppermute | solution.py:12
  53.1 4.2 %collective-permute-done.5 = bf16[2,2,128,512]{3,2,1,0:T(8,128)(2,1)S(1)} collective-permute-done((bf16[2,2,128,512]{3,2,1,0:T(8,128)(2,1)S(1)}, bf16[2,2,128,512]{3,2,1,0:T(8,128)(2,1)S(1)}, u32[]{:S(2)}, u32[]{:S(2)}) %collective-permute-start.5) | collective-permute-done | bytes 524320 | tf_op jit(solution)/shard_map/ppermute | solution.py:12
  58.1 2.7 %gather_fusion = bf16[8,2,128,512]{3,2,1,0:T(8,128)(2,1)S(1)} fusion(bf16[2,14,128,512]{3,2,1,0:T(8,128)(2,1)} %constant_dynamic-update-slice_fusion, s32[1024]{0:T(1024)S(1)} %pad_clamp_fusion.1), kind=kCustom, calls=%fused_computation.clone | custom fusion | bytes 4194336 | tf_op jit(solution)/shard_map/jit(_take)/gather | solution.py:47
  60.8 4.0 %gather_fusion.1 = bf16[8,2,128,512]{3,2,1,0:T(8,128)(2,1)} fusion(bf16[2,14,128,512]{3,2,1,0:T(8,128)(2,1)} %constant_dynamic-update-slice_fusion, s32[1024]{0:T(1024)S(1)} %pad_clamp_fusion), kind=kCustom, calls=%fused_computation.1.clone | custom fusion | bytes 4194336 | tf_op jit(solution)/shard_map/jit(_take)/gather | solution.py:47
  64.9 2.0 select_bitcast_fusion
  68.2 1.4 convert_element_type.10
  74.3 1.5 pad_maximum_fusion.2
  75.7 9.9 %all-reduce.1 = bf16[2,2,128,8,128]{4,3,2,1,0:T(8,128)(2,1)} all-reduce(f32[2,2,128,8,128]{4,3,2,1,0:T(8,128)} %pad_maximum_fusion.2), channel_id=1, replica_groups=mesh['freq'=2,'tile'=8,'src'=2] {'src'}, use_global_device_ids=true, to_apply=%region_1.0 | all-reduce | flops 524288 | bytes 3145728 | tf_op jit(solution)/shard_map/psum | solution.py:59
  85.6 1.3 fusion.60
  89.7 1.6 fusion.25
  92.7 2.3 %pad_maximum_fusion = f32[1024,2,512]{0,2,1:T(8,128)} fusion(f32[1024,1,512]{0,2,1:T(8,128)S(1)} %subtract_bitcast_fusion, f32[1024,1,512]{0,2,1:T(8,128)S(1)} %add_bitcast_fusion), kind=kLoop, calls=%fused_computation.2 | loop fusion | flops 1048576 | bytes 8388608 | tf_op jit(solution)/shard_map/stack | solution.py:81
  95.0 106.2 %reduce-scatter.5.cloned.1.call-done = f32[128,2,512]{0,2,1:T(8,128)} async-done(((f32[1024,2,512]{0,2,1:T(8,128)}), f32[128,2,512]{0,2,1:T(8,128)}) %reduce-scatter.5.cloned.1.call-update) | async-done | bytes 524304 | tf_op jit(solution)/shard_map/reduce_scatter | solution.py:80
  201.2 2.0 copy.5
  (69 shorter events, 18.7 us)
Async XLA Ops:
  6.5 2.0 copy-start.2
  6.5 3.4 %copy-start.3 = (bf16[2,256,512]{2,1,0:T(8,128)(2,1)S(1)}, bf16[2,256,512]{2,1,0:T(8,128)(2,1)}, u32[]{:S(2)}) copy-start(bf16[2,256,512]{2,1,0:T(8,128)(2,1)} %param.6) | copy-start | bytes 1572868
  6.5 61.6 %reduce-scatter.3.cloned.1.call-start = ((), (), s32[]{:S(2)}) async-start(), calls=%async_computation.2 | async-start | bytes 3145728 | tf_op jit(solution)/shard_map/reduce_scatter | solution.py:26
  12.3 15.8 %copy-start.6 = (s32[2,8]{1,0:T(2,128)S(1)}, s32[2,8]{1,0:T(2,128)}, u32[]{:S(2)}) copy-start(s32[2,8]{1,0:T(2,128)} %param.8) | copy-start | bytes 196
  12.3 15.8 %copy-start.7 = (s32[2]{0:T(128)S(1)}, s32[2]{0:T(128)}, u32[]{:S(2)}) copy-start(s32[2]{0:T(128)} %param.9) | copy-start | bytes 28
  12.3 18.4 %copy-start.4 = (bf16[2,256,512]{2,1,0:T(8,128)(2,1)S(1)}, bf16[2,256,512]{2,1,0:T(8,128)(2,1)}, u32[]{:S(2)}) copy-start(bf16[2,256,512]{2,1,0:T(8,128)(2,1)} %param.6) | copy-start | bytes 1572868
  12.3 77.4 %all-gather.2.cloned.1.call-start = ((), (), s32[]{:S(2)}) async-start(), calls=%async_computation.3 | async-start | bytes 1572864 | tf_op jit(solution)/shard_map/all_gather | solution.py:72
  12.4 18.4 %collective-permute-start = (bf16[2,2,128,512]{3,2,1,0:T(8,128)(2,1)S(1)}, bf16[2,2,128,512]{3,2,1,0:T(8,128)(2,1)}, u32[]{:S(2)}, u32[]{:S(2)}) collective-permute-start(bf16[2,2,128,512]{3,2,1,0:T(8,128)(2,1)S(1)} %bitcast.167), channel_id=1, source_target_pairs={{0,6},{2,8},{4,10},{6,12},{8,14},{1,7},{3,9},{5,11},{7,13},{9,15},... | collective-permute-start | bytes 1572872 | tf_op jit(solution)/shard_map/ppermute | solution.py:12
  19.2 21.6 %collective-permute-start.1 = (bf16[2,2,128,512]{3,2,1,0:T(8,128)(2,1)S(1)}, bf16[2,2,128,512]{3,2,1,0:T(8,128)(2,1)S(1)}, u32[]{:S(2)}, u32[]{:S(2)}) collective-permute-start(bf16[2,2,128,512]{3,2,1,0:T(8,128)(2,1)S(1)} %bitcast.168), channel_id=1, source_target_pairs={{0,4},{2,6},{4,8},{6,10},{8,12},{10,14},{1,5},{3,7},{5,9},{7,11},{... | collective-permute-start | bytes 1572872 | tf_op jit(solution)/shard_map/ppermute | solution.py:12
  22.7 24.5 %collective-permute-start.2 = (bf16[2,2,128,512]{3,2,1,0:T(8,128)(2,1)S(1)}, bf16[2,2,128,512]{3,2,1,0:T(8,128)(2,1)S(1)}, u32[]{:S(2)}, u32[]{:S(2)}) collective-permute-start(bf16[2,2,128,512]{3,2,1,0:T(8,128)(2,1)S(1)} %bitcast.169), channel_id=1, source_target_pairs={{0,2},{2,4},{4,6},{6,8},{8,10},{10,12},{12,14},{1,3},{3,5},{5,7},{... | collective-permute-start | bytes 1572872 | tf_op jit(solution)/shard_map/ppermute | solution.py:12
  25.4 23.5 %collective-permute-start.3 = (bf16[2,2,128,512]{3,2,1,0:T(8,128)(2,1)S(1)}, bf16[2,2,128,512]{3,2,1,0:T(8,128)(2,1)S(1)}, u32[]{:S(2)}, u32[]{:S(2)}) collective-permute-start(bf16[2,2,128,512]{3,2,1,0:T(8,128)(2,1)S(1)} %bitcast.170), channel_id=1, source_target_pairs={{2,0},{4,2},{6,4},{8,6},{10,8},{12,10},{14,12},{3,1},{5,3},{7,5},{... | collective-permute-start | bytes 1572872 | tf_op jit(solution)/shard_map/ppermute | solution.py:12
  26.7 25.6 %collective-permute-start.4 = (bf16[2,2,128,512]{3,2,1,0:T(8,128)(2,1)S(1)}, bf16[2,2,128,512]{3,2,1,0:T(8,128)(2,1)S(1)}, u32[]{:S(2)}, u32[]{:S(2)}) collective-permute-start(bf16[2,2,128,512]{3,2,1,0:T(8,128)(2,1)S(1)} %bitcast.171), channel_id=1, source_target_pairs={{4,0},{6,2},{8,4},{10,6},{12,8},{14,10},{5,1},{7,3},{9,5},{11,7},{... | collective-permute-start | bytes 1572872 | tf_op jit(solution)/shard_map/ppermute | solution.py:12
  28.1 173.1 %reduce-scatter.5.cloned.1.call-start = ((), (), s32[]{:S(2)}) async-start(), calls=%async_computation.4 | async-start | bytes 4718592 | tf_op jit(solution)/shard_map/reduce_scatter | solution.py:80
  30.8 26.5 %collective-permute-start.5 = (bf16[2,2,128,512]{3,2,1,0:T(8,128)(2,1)S(1)}, bf16[2,2,128,512]{3,2,1,0:T(8,128)(2,1)S(1)}, u32[]{:S(2)}, u32[]{:S(2)}) collective-permute-start(bf16[2,2,128,512]{3,2,1,0:T(8,128)(2,1)S(1)} %bitcast.172), channel_id=1, source_target_pairs={{6,0},{8,2},{10,4},{12,6},{14,8},{7,1},{9,3},{11,5},{13,7},{15,9},... | collective-permute-start | bytes 1572872 | tf_op jit(solution)/shard_map/ppermute | solution.py:12
  68.2 1.5 copy-start
  85.6 1.5 copy-start.1
  89.7 1.6 copy-start.5
Sparse Core Ops, SparseCore 0:
  12.5 12.3 reduce-scatter.2
  28.2 11.3 all-gather.1
  95.1 106.0 reduce-scatter.4
where the time goes:
time: 210 us
  waiting for transfers between devices  128 us (61%)
  local copies, waits for them, and re-layouts  19.1 us (9%)
  starting transfers between devices  17 us (8%)
  between operations  13.5 us (6%)
  matrix products  13.3 us (6%)
  blocking collectives  9.88 us (5%)
  other arithmetic  9.03 us (4%)
    reduce_scatter x1, waiting for transfers between devices, shards(): lax.psum_scatter(jnp.stack([out_real, out_imag], axis=1), 'tile', scatter...  106 us
    ppermute x6, waiting for transfers between devices, from_behind(): lax.ppermute(value, axis, [(source, source + steps) for source in range(f...  21.7 us
    ppermute x6, starting transfers between devices, from_behind(): lax.ppermute(value, axis, [(source, source + steps) for source in range(f...  16.9 us
    psum x1, blocking collectives, shards(): coupling = lax.psum(partial_blocks, 'src').astype(jnp.bfloat16)  9.88 us
    unnamed x26, local copies, waits for them, and re-layouts  6.92 us
    gather x2, local copies, waits for them, and re-layouts, shards(): jnp.take(window, local_index[row], axis=1).reshape(2, kmax * tile, half)  6.74 us
  transfers between devices with their start and end apart: 9, of which 6 were waited for; matrix products, arithmetic and copies ran while one was open for 13% of the time, Pallas kernels for 0%

commit v1 on v0

v1 whole, which is shorter than its diff:
```python
import functools

import jax
import jax.numpy as jnp
from jax import lax
from jax.experimental import pallas as pl
from jax.experimental.pallas import tpu as pltpu
from jax.sharding import PartitionSpec as P

BAND_DEV = 3
PIECES = 4
CHUNKS = 2
OWN, ACROSS, NEAR, BACK, BACK_ACROSS, NEAR_ACROSS, FAR, PAIR, PAIR_ACROSS = range(9)
OFFSETS = (0, 1, 2, -2, -1, 3, -3)
ROUTES = (
    (OWN, ACROSS),
    (OWN, BACK),
    (OWN, NEAR),
    (ACROSS, NEAR_ACROSS),
    (NEAR, BACK_ACROSS),
    (BACK_ACROSS, FAR),
)
F32 = jnp.float32
BF16 = jnp.bfloat16


def dot(left, right, dims):
    return lax.dot_general(left, right, (dims, ((), ())), preferred_element_type=F32)


def kernel(
    count_tile, a_ref, v_ref, mask_ref, out_ref,
    win, vbuf, img, ipart, irecv, cpart, crecv, acc, w, rr, hp, hr,
    load_sem, img_sem, route_send, route_recv, couple_send, couple_recv,
    pair_send, pair_recv, w_send, w_recv, h_send, h_recv,
):
    me = lax.axis_index("tile")
    core = lax.axis_index("src")
    side = lax.rem(me, 2)
    level = me // 2
    levels = count_tile // 2
    step = 1 - 2 * side
    rows, half = win.shape[2], win.shape[3]
    tiles = mask_ref.shape[1]
    out_rows = out_ref.shape[1]
    wide = half // CHUNKS

    def inside(place):
        return (place >= 0) & (place < levels)

    has_near = inside(level + step)
    has_back = inside(level - step)
    has_far = inside(level - 2 * step)
    across = {"tile": me + step}
    forward = {"tile": me + 2 * step}
    backward = {"tile": me - 2 * step}
    partner = {"src": 1 - core}
    targets = (across, forward, backward, backward, across, forward)
    sends = (None, has_near, has_back, has_back, has_near, has_near & has_back)
    arrives = (None, has_back, has_near, has_near, has_back, has_far)

    def guarded(condition, run):
        if condition is None:
            run()
        else:
            pl.when(condition)(run)

    def remote(source, target, send, recv, device):
        return pltpu.make_async_remote_copy(
            src_ref=source, dst_ref=target, send_sem=send, recv_sem=recv,
            device_id=device, device_id_type=pl.DeviceIdType.MESH,
        )

    def piece(slot, index):
        depth = 2 * rows // PIECES
        per = PIECES // 2
        return win.at[slot, index // per, pl.ds((index % per) * depth, depth)]

    def route(number, index):
        source, target = ROUTES[number]
        return remote(
            piece(source, index), piece(target, index),
            route_send.at[number, index], route_recv.at[number, index], targets[number],
        )

    def send_route(number, index):
        guarded(sends[number], lambda: route(number, index).start())

    def arrive(number, index):
        guarded(arrives[number], lambda: route(number, index).wait_recv())

    def to_pair(source, target, number):
        return remote(win.at[source], win.at[target], pair_send.at[number], pair_recv.at[number], partner)

    load_a = pltpu.make_async_copy(a_ref, win.at[OWN], load_sem.at[0])
    load_theirs = pltpu.make_async_copy(
        v_ref.at[:, :, pl.ds(pl.multiple_of((1 - core) * half, half), half)], vbuf.at[0], load_sem.at[1]
    )
    load_mine = pltpu.make_async_copy(
        v_ref.at[:, :, pl.ds(pl.multiple_of(core * half, half), half)], vbuf.at[1], load_sem.at[2]
    )
    load_a.start()
    load_theirs.start()
    load_mine.start()

    barrier = pltpu.get_barrier_semaphore()
    pl.semaphore_signal(barrier, inc=1, device_id=partner, device_id_type=pl.DeviceIdType.MESH)
    pl.semaphore_signal(barrier, inc=1, device_id=across, device_id_type=pl.DeviceIdType.MESH)

    def other_level(number):
        return lax.rem(level + 1 + number, levels)

    @pl.loop(0, levels - 1)
    def _(number):
        pl.semaphore_signal(
            barrier, inc=1, device_id={"tile": other_level(number) * 2 + side},
            device_id_type=pl.DeviceIdType.MESH,
        )

    pl.semaphore_wait(barrier, levels + 1)
    load_a.wait()
    for index in range(PIECES):
        for number in (0, 1, 2):
            send_route(number, index)
    to_pair(OWN, PAIR, 0).start()

    own = win[OWN].reshape(2 * rows, half)

    def images(slot):
        first = dot(own, vbuf[slot, 0], ((1,), (0,)))
        second = dot(own, vbuf[slot, 1], ((1,), (0,)))
        return first[:rows] - second[rows:], second[:rows] + first[rows:]

    load_theirs.wait()
    real, imag = images(0)
    ipart[0] = real
    ipart[1] = imag
    image_copy = remote(ipart, irecv, img_sem.at[0], img_sem.at[1], partner)
    image_copy.start()
    load_mine.wait()
    real, imag = images(1)
    image_copy.wait_recv()
    img[:rows] = (real + irecv[0]).astype(BF16)
    img[rows:] = (imag + irecv[1]).astype(BF16)

    acc[...] = jnp.zeros_like(acc)

    def exists(slot):
        return (
            (slot <= ACROSS)
            | (((slot == NEAR) | (slot == NEAR_ACROSS)) & has_near)
            | (((slot == BACK) | (slot == BACK_ACROSS)) & has_back)
            | ((slot == FAR) & has_far)
        )

    def couple_copy(slot):
        return remote(cpart.at[slot], crecv.at[slot], couple_send.at[slot], couple_recv.at[slot], partner)

    def couple(low, high):
        @pl.loop(low, high)
        def _(slot):
            @pl.when(exists(slot))
            def _():
                block = win[slot].reshape(2 * rows, half)
                prod = dot(img[...], block, ((1,), (1,)))
                cpart[slot, 0] = prod[:rows, :rows] + prod[rows:, rows:]
                cpart[slot, 1] = prod[rows:, :rows] - prod[:rows, rows:]
                couple_copy(slot).start()

    def weigh(low, high):
        @pl.loop(low, high)
        def _(slot):
            @pl.when(exists(slot))
            def _():
                couple_copy(slot).wait_recv()
                live = jnp.concatenate(
                    [jnp.broadcast_to(mask_ref[slot, row], (rows // tiles, rows)) for row in range(tiles)], axis=0
                )
                real = ((cpart[slot, 0] + crecv[slot, 0]) * live).astype(BF16)
                imag = ((cpart[slot, 1] + crecv[slot, 1]) * live).astype(BF16)
                left = jnp.concatenate(
                    [jnp.concatenate([real, -imag], axis=1), jnp.concatenate([imag, real], axis=1)], axis=0
                )
                acc[...] += dot(left, win[slot].reshape(2 * rows, half), ((1,), (0,)))

    def pass_on(index):
        arrive(0, index)
        send_route(3, index)
        arrive(2, index)
        send_route(4, index)

    couple(OWN, ACROSS)
    for index in range(PIECES):
        pass_on(index)
    to_pair(ACROSS, PAIR_ACROSS, 1).start()
    for index in range(PIECES):
        arrive(1, index)
    couple(ACROSS, BACK_ACROSS)
    weigh(OWN, BACK_ACROSS)
    for index in range(PIECES):
        arrive(4, index)
        send_route(5, index)
    for index in range(PIECES):
        arrive(3, index)
    couple(BACK_ACROSS, FAR)
    weigh(BACK_ACROSS, FAR)
    for index in range(PIECES):
        arrive(5, index)
    couple(FAR, FAR + 1)
    weigh(FAR, FAR + 1)

    def w_copy(chunk):
        return remote(w.at[chunk, 0], w.at[chunk, 1], w_send.at[chunk], w_recv.at[chunk], across)

    for chunk in range(CHUNKS):
        w[chunk, 0] = acc[:, chunk * wide : (chunk + 1) * wide].astype(BF16)
        w_copy(chunk).start()
    to_pair(OWN, PAIR, 0).wait_recv()
    to_pair(ACROSS, PAIR_ACROSS, 1).wait_recv()

    span = max(out_rows, 128)

    def fill(chunk, group):
        if span == out_rows:
            column = (2 * group + side) * out_rows
        else:
            column = group * span
        which = column // half
        base = jnp.where(which == core, OWN, PAIR)
        lanes = pl.ds(pl.multiple_of(column - which * half, 128), span)
        total = dot(win[base, :, :, lanes].reshape(2 * rows, span), rr[0], ((0,), (0,)))
        total += dot(win[base + 1, :, :, lanes].reshape(2 * rows, span), rr[1], ((0,), (0,)))
        hp[chunk, pl.ds(pl.multiple_of(column, span), span)] = total.astype(BF16)

    def term(chunk, target, sender):
        first = pl.multiple_of((2 * target + side) * out_rows, out_rows)
        return remote(
            hp.at[chunk, pl.ds(first, out_rows)], hr.at[chunk, sender],
            h_send.at[chunk, target], h_recv.at[chunk, sender], {"tile": 2 * target + side},
        )

    for chunk in range(CHUNKS):
        w_copy(chunk).wait_recv()
        for block in range(2):
            top, low = w[chunk, block, :rows], w[chunk, block, rows:]
            rr[block, :rows] = jnp.concatenate([top, low], axis=1)
            rr[block, rows:] = jnp.concatenate([low, -top], axis=1)
        if span != out_rows:
            @pl.loop(0, hp.shape[1] // span)
            def _(group):
                fill(chunk, group)

        @pl.loop(0, levels - 1)
        def _(number):
            target = other_level(number)
            if span == out_rows:
                fill(chunk, target)
            term(chunk, target, level).start()

        if span == out_rows:
            fill(chunk, level)

    mine = pl.ds(pl.multiple_of((2 * level + side) * out_rows, out_rows), out_rows)
    for chunk in range(CHUNKS):
        def add(number, total):
            sender = other_level(number)
            term(chunk, level, sender).wait_recv()
            return total + hr[chunk, sender].astype(F32)

        total = lax.fori_loop(0, levels - 1, add, hp[chunk, mine].astype(F32))
        out_ref[0, :, chunk * wide : (chunk + 1) * wide] = total[:, :wide]
        out_ref[1, :, chunk * wide : (chunk + 1) * wide] = total[:, wide:]

    for number in range(len(ROUTES)):
        for index in range(PIECES):
            guarded(sends[number], lambda number=number, index=index: route(number, index).wait_send())
    to_pair(OWN, PAIR, 0).wait_send()
    to_pair(ACROSS, PAIR_ACROSS, 1).wait_send()
    image_copy.wait_send()

    @pl.loop(0, FAR + 1)
    def _(slot):
        @pl.when(exists(slot))
        def _():
            couple_copy(slot).wait_send()

    for chunk in range(CHUNKS):
        w_copy(chunk).wait_send()

        @pl.loop(0, levels - 1)
        def _(number):
            term(chunk, other_level(number), level).wait_send()


def shards(count_tile, green, direction, partners, counts):
    tile_dev, kmax = partners.shape
    rows, half = green.shape[1:]
    tile = rows // tile_dev
    sources = direction.shape[2]
    out_rows = sources // count_tile
    levels = count_tile // 2
    wide = half // CHUNKS
    me = lax.axis_index("tile")
    step = 1 - 2 * (me % 2)
    offsets = jnp.array(OFFSETS, jnp.int32) * step
    block_tiles = (me + offsets)[:, None] * tile_dev + jnp.arange(tile_dev, dtype=jnp.int32)[None, :]
    live = jnp.arange(kmax, dtype=jnp.int32)[None, :] < counts[:, None]
    hit = (partners[None, :, None, :] == block_tiles[:, None, :, None]) & live[None, :, None, :]
    mask = jnp.repeat(jnp.any(hit, axis=3).astype(F32), tile, axis=2)[:, :, None, :]
    anywhere = pl.BlockSpec(memory_space=pl.ANY)
    local = pl.BlockSpec(memory_space=pltpu.VMEM)
    dma = pltpu.SemaphoreType.DMA
    out = pl.pallas_call(
        functools.partial(kernel, count_tile),
        out_shape=jax.ShapeDtypeStruct((2, out_rows, half), F32),
        in_specs=[anywhere, anywhere, local],
        out_specs=local,
        scratch_shapes=[
            pltpu.VMEM((9, 2, rows, half), BF16),
            pltpu.VMEM((2, 2, half, half), BF16),
            pltpu.VMEM((2 * rows, half), BF16),
            pltpu.VMEM((2, rows, half), F32),
            pltpu.VMEM((2, rows, half), F32),
            pltpu.VMEM((FAR + 1, 2, rows, rows), F32),
            pltpu.VMEM((FAR + 1, 2, rows, rows), F32),
            pltpu.VMEM((2 * rows, half), F32),
            pltpu.VMEM((CHUNKS, 2, 2 * rows, wide), BF16),
            pltpu.VMEM((2, 2 * rows, 2 * wide), BF16),
            pltpu.VMEM((CHUNKS, sources, 2 * wide), BF16),
            pltpu.VMEM((CHUNKS, levels, out_rows, 2 * wide), BF16),
            dma((3,)),
            dma((2,)),
            dma((len(ROUTES), PIECES)),
            dma((len(ROUTES), PIECES)),
            dma((FAR + 1,)),
            dma((FAR + 1,)),
            dma((2,)),
            dma((2,)),
            dma((CHUNKS,)),
            dma((CHUNKS,)),
            dma((CHUNKS, levels)),
            dma((CHUNKS, levels)),
        ],
        compiler_params=pltpu.CompilerParams(
            collective_id=0, has_side_effects=True, vmem_limit_bytes=56 * 1024 * 1024
        ),
    )(green, direction, mask)
    return jnp.swapaxes(out, 0, 1)


def solution(mesh):
    in_specs = (
        P(None, ("freq", "tile"), "src"),
        P(None, ("freq", "src"), None),
        P(("freq", "tile"), None),
        P(("freq", "tile")),
    )
    out_specs = P(("freq", "tile"), None, "src")
    body = functools.partial(shards, mesh.shape["tile"])
    return jax.shard_map(body, mesh=mesh, in_specs=in_specs, out_specs=out_specs, check_vma=False)
```

time: 210 us -> 76.5 us (0.36)
  the two profiles are of different devices: /device:TPU:0 before, /device:TPU:11 now
where the time goes in v1:
time: 76.5 us; the launch traced here: 76.2 us
  Pallas kernels  70.9 us (93%)
  local copies, waits for them, and re-layouts  3.03 us (4%)
  other arithmetic  2.29 us (3%)
    pallas_call x1, Pallas kernels, shards(): pl.pallas_call(functools.partial(kernel, count_tile), out_shape=jax.Shape...  70.9 us
    transpose x1, local copies, waits for them, and re-layouts, shards(): return jnp.swapaxes(out, 0, 1)  2.24 us

profile of v1, /device:TPU:11, one launch (start us, length us, event | category | flops | bytes accessed | tf_op | source)
XLA Modules:
  0.0 76.2 jit_solution(9371571401289851342)
XLA Ops:
  0.0 0.7 add_multiply_fusion
  0.7 0.7 iota_compare_fusion
  1.4 0.9 %and_reduce_fusion = pred[7,2,2]{0,2,1:T(4,128)(4,1)S(1)} fusion(s32[7,2]{0,1:T(2,128)S(1)} %iota_add_fusion, s32[2,8]{1,0:T(2,128)} %param.7, pred[2,8]{1,0:T(4,128)(4,1)S(1)} %iota_compare_fusion), kind=kLoop, calls=%fused_computation | loop fusion | flops 644 | bytes 164 | tf_op jit(solution)/shard_map/reduce_or | solution.py:309
  2.3 0.1 copy.7
  2.4 0.7 broadcast_in_dim.2
  3.1 70.9 %shard_map.55 = f32[2,128,512]{2,1,0:T(8,128)} custom-call(bf16[2,256,512]{2,1,0:T(8,128)(2,1)} %a_ref.1, bf16[2,512,1024]{2,1,0:T(8,128)(2,1)} %v_ref.1, f32[7,2,1,256]{3,2,1,0:T(1,128)} %bitcast.3), custom_call_target="tpu_custom_call" | custom-call | tf_op jit(solution)/shard_map/pallas_call | solution.py:313
  74.0 2.2 %copy.8 = f32[128,2,512]{2,1,0:T(2,128)} copy(f32[128,2,512]{2,0,1:T(8,128)} %bitcast.2) | data formatting | bytes 1048576 | tf_op jit(solution)/shard_map/transpose | solution.py:348
  (2 shorter events, 0.0 us)

commit v2 on v1

--- a/solution.py
+++ b/solution.py
@@ -9,7 +9,7 @@
 
 BAND_DEV = 3
 PIECES = 4
-CHUNKS = 2
+CHUNKS = 4
 OWN, ACROSS, NEAR, BACK, BACK_ACROSS, NEAR_ACROSS, FAR, PAIR, PAIR_ACROSS = range(9)
 OFFSETS = (0, 1, 2, -2, -1, 3, -3)
 ROUTES = (
@@ -28,11 +28,15 @@
     return lax.dot_general(left, right, (dims, ((), ())), preferred_element_type=F32)
 
 
+def short_line(out_rows, levels):
+    return out_rows % 128 == 0 and levels <= 4
+
+
 def kernel(
-    count_tile, a_ref, v_ref, mask_ref, out_ref,
-    win, vbuf, img, ipart, irecv, cpart, crecv, acc, w, rr, hp, hr,
+    count_tile, a_ref, v_ref, partners_ref, counts_ref, out_ref,
+    table, sampled, win, vbuf, img, ipart, irecv, cpart, crecv, acc, w, turned, rr, hp, hr,
     load_sem, img_sem, route_send, route_recv, couple_send, couple_recv,
-    pair_send, pair_recv, w_send, w_recv, h_send, h_recv,
+    pair_send, pair_recv, w_send, w_recv, h_send, h_recv, o_send,
 ):
     me = lax.axis_index("tile")
     core = lax.axis_index("src")
@@ -41,8 +45,8 @@
     levels = count_tile // 2
     step = 1 - 2 * side
     rows, half = win.shape[2], win.shape[3]
-    tiles = mask_ref.shape[1]
-    out_rows = out_ref.shape[1]
+    tiles, kmax = table.shape
+    out_rows = out_ref.shape[0]
     wide = half // CHUNKS
 
     def inside(place):
@@ -99,7 +103,11 @@
     load_mine = pltpu.make_async_copy(
         v_ref.at[:, :, pl.ds(pl.multiple_of(core * half, half), half)], vbuf.at[1], load_sem.at[2]
     )
+    load_table = pltpu.make_async_copy(partners_ref, table, load_sem.at[3])
+    load_counts = pltpu.make_async_copy(counts_ref, sampled, load_sem.at[4])
     load_a.start()
+    load_table.start()
+    load_counts.start()
     load_theirs.start()
     load_mine.start()
 
@@ -143,6 +151,8 @@
     img[:rows] = (real + irecv[0]).astype(BF16)
     img[rows:] = (imag + irecv[1]).astype(BF16)
 
+    load_table.wait()
+    load_counts.wait()
     acc[...] = jnp.zeros_like(acc)
 
     def exists(slot):
@@ -152,6 +162,23 @@
             | (((slot == BACK) | (slot == BACK_ACROSS)) & has_back)
             | ((slot == FAR) & has_far)
         )
+
+    def sample(slot):
+        offset = 0
+        for index, value in enumerate(OFFSETS):
+            offset = jnp.where(slot == index, value, offset)
+        first = (me + offset * step) * tiles
+        tile = rows // tiles
+        bands = []
+        for row in range(tiles):
+            blocks = []
+            for column in range(tiles):
+                hit = False
+                for k in range(kmax):
+                    hit = hit | ((table[row, k] == first + column) & (k < sampled[row]))
+                blocks.append(jnp.full((tile, tile), jnp.where(hit, 1.0, 0.0), F32))
+            bands.append(jnp.concatenate(blocks, axis=1))
+        return jnp.concatenate(bands, axis=0)
 
     def couple_copy(slot):
         return remote(cpart.at[slot], crecv.at[slot], couple_send.at[slot], couple_recv.at[slot], partner)
@@ -173,9 +200,7 @@
             @pl.when(exists(slot))
             def _():
                 couple_copy(slot).wait_recv()
-                live = jnp.concatenate(
-                    [jnp.broadcast_to(mask_ref[slot, row], (rows // tiles, rows)) for row in range(tiles)], axis=0
-                )
+                live = sample(slot)
                 real = ((cpart[slot, 0] + crecv[slot, 0]) * live).astype(BF16)
                 imag = ((cpart[slot, 1] + crecv[slot, 1]) * live).astype(BF16)
                 left = jnp.concatenate(
@@ -195,19 +220,41 @@
     to_pair(ACROSS, PAIR_ACROSS, 1).start()
     for index in range(PIECES):
         arrive(1, index)
-    couple(ACROSS, BACK_ACROSS)
-    weigh(OWN, BACK_ACROSS)
-    for index in range(PIECES):
+    span = max(out_rows, 128)
+
+    def turn_over():
+        to_pair(OWN, PAIR, 0).wait_recv()
+        to_pair(ACROSS, PAIR_ACROSS, 1).wait_recv()
+
+        @pl.loop(0, turned.shape[0])
+        def _(group):
+            column = (2 * group + side) * out_rows if span == out_rows else group * span
+            which = column // half
+            base = jnp.where(which == core, OWN, PAIR)
+            lanes = pl.ds(pl.multiple_of(column - which * half, 128), span)
+            for block in range(2):
+                turned[group, :, block * 2 * rows : (block + 1) * 2 * rows] = (
+                    win[base + block, :, :, lanes].reshape(2 * rows, span).T
+                )
+
+    jobs = (
+        lambda: couple(ACROSS, BACK_ACROSS),
+        lambda: weigh(OWN, NEAR),
+        lambda: weigh(NEAR, BACK_ACROSS),
+        turn_over,
+    )
+    for index in range(PIECES):
+        for job in jobs[index * len(jobs) // PIECES : (index + 1) * len(jobs) // PIECES]:
+            job()
         arrive(4, index)
         send_route(5, index)
     for index in range(PIECES):
         arrive(3, index)
     couple(BACK_ACROSS, FAR)
-    weigh(BACK_ACROSS, FAR)
     for index in range(PIECES):
         arrive(5, index)
     couple(FAR, FAR + 1)
-    weigh(FAR, FAR + 1)
+    weigh(BACK_ACROSS, FAR + 1)
 
     def w_copy(chunk):
         return remote(w.at[chunk, 0], w.at[chunk, 1], w_send.at[chunk], w_recv.at[chunk], across)
@@ -215,61 +262,133 @@
     for chunk in range(CHUNKS):
         w[chunk, 0] = acc[:, chunk * wide : (chunk + 1) * wide].astype(BF16)
         w_copy(chunk).start()
-    to_pair(OWN, PAIR, 0).wait_recv()
-    to_pair(ACROSS, PAIR_ACROSS, 1).wait_recv()
-
-    span = max(out_rows, 128)
-
-    def fill(chunk, group):
-        if span == out_rows:
-            column = (2 * group + side) * out_rows
-        else:
-            column = group * span
-        which = column // half
-        base = jnp.where(which == core, OWN, PAIR)
-        lanes = pl.ds(pl.multiple_of(column - which * half, 128), span)
-        total = dot(win[base, :, :, lanes].reshape(2 * rows, span), rr[0], ((0,), (0,)))
-        total += dot(win[base + 1, :, :, lanes].reshape(2 * rows, span), rr[1], ((0,), (0,)))
-        hp[chunk, pl.ds(pl.multiple_of(column, span), span)] = total.astype(BF16)
-
-    def term(chunk, target, sender):
-        first = pl.multiple_of((2 * target + side) * out_rows, out_rows)
-        return remote(
-            hp.at[chunk, pl.ds(first, out_rows)], hr.at[chunk, sender],
-            h_send.at[chunk, target], h_recv.at[chunk, sender], {"tile": 2 * target + side},
-        )
-
-    for chunk in range(CHUNKS):
+    def partial(chunk, group):
+        return dot(turned[group], rr[chunk], ((1,), (0,)))
+
+    def rows_of(target):
+        return pl.multiple_of((2 * target + side) * out_rows, out_rows)
+
+    def prepare(chunk):
         w_copy(chunk).wait_recv()
         for block in range(2):
             top, low = w[chunk, block, :rows], w[chunk, block, rows:]
-            rr[block, :rows] = jnp.concatenate([top, low], axis=1)
-            rr[block, rows:] = jnp.concatenate([low, -top], axis=1)
-        if span != out_rows:
-            @pl.loop(0, hp.shape[1] // span)
-            def _(group):
-                fill(chunk, group)
-
-        @pl.loop(0, levels - 1)
-        def _(number):
-            target = other_level(number)
+            first = 2 * rows * block
+            rr[chunk, first : first + rows] = jnp.concatenate([top, low], axis=1)
+            rr[chunk, first + rows : first + 2 * rows] = jnp.concatenate([low, -top], axis=1)
+
+    def put(chunk, total, more=False):
+        for part in range(2):
+            for index in range(wide // 128):
+                place = 2 * (chunk * wide // 128 + index) + part
+                first = part * wide + index * 128
+                value = total[:, first : first + 128]
+                out_ref[:, place] = out_ref[:, place] + value if more else value
+
+    def term(chunk, lane, slot, target, level_to):
+        return remote(
+            hp.at[chunk, pl.ds(rows_of(target), out_rows)], hr.at[chunk, lane, slot],
+            h_send.at[chunk, target], h_recv.at[chunk, lane, slot], {"tile": 2 * level_to + side},
+        )
+
+    def onward(chunk, lane, target):
+        return remote(
+            hr.at[chunk, lane, target], hr.at[chunk, lane, target],
+            o_send.at[chunk], h_recv.at[chunk, lane, target], {"tile": 2 * target + side},
+        )
+
+    if short_line(out_rows, levels):
+        def flow(turn, first):
+            lane = jnp.where(2 * level < levels, 1 - first, first)
+            depth = jnp.where(lane == 0, level, levels - 1 - level)
+            chunk = turn - jnp.maximum(depth - 1, 0)
+
+            @pl.when((chunk >= 0) & (chunk < CHUNKS))
+            def _():
+                @pl.loop(0, levels - 1 - depth - jnp.where(depth == 0, 1, 0))
+                def _(number):
+                    target = jnp.where(lane == 0, levels - 1 - number, number)
+                    total = partial(chunk, target)
+                    passing = term(chunk, lane, target, target, level + 1 - 2 * lane)
+                    place = pl.ds(rows_of(target), out_rows)
+
+                    @pl.when(depth == 0)
+                    def _():
+                        hp[chunk, place] = total.astype(BF16)
+
+                    @pl.when(depth == 1)
+                    def _():
+                        passing.wait_recv()
+                        hp[chunk, place] = (total + hr[chunk, lane, target].astype(F32)).astype(BF16)
+
+                    @pl.when(depth <= 1)
+                    def _():
+                        passing.start()
+
+                    @pl.when(depth > 1)
+                    def _():
+                        passing.wait_recv()
+                        onward(chunk, lane, target).start()
+                        hp[chunk, place] = total.astype(BF16)
+                        term(chunk, lane, levels, target, target).start()
+
+        @pl.loop(0, CHUNKS + max(levels - 3, 0))
+        def _(turn):
+            @pl.when(turn < CHUNKS)
+            def _():
+                prepare(turn)
+
+            flow(turn, 0)
+            flow(turn, 1)
+
+        @pl.when((level == 0) | (level == levels - 1))
+        def _():
+            lane = jnp.where(level == 0, 0, 1)
+            target = level + 1 - 2 * lane
+
+            @pl.loop(0, CHUNKS)
+            def _(chunk):
+                hp[chunk, pl.ds(rows_of(target), out_rows)] = partial(chunk, target).astype(BF16)
+                term(chunk, lane, target, target, target).start()
+
+        for chunk in range(CHUNKS):
+            put(chunk, partial(chunk, level))
+        for chunk in range(CHUNKS):
+            before = level, levels - 1 - level
+            for lane, slot, there in (
+                (0, level, before[0] > 0), (1, level, before[1] > 0),
+                (0, levels, before[0] > 2), (1, levels, before[1] > 2),
+            ):
+                @pl.when(there)
+                def _(chunk=chunk, lane=lane, slot=slot):
+                    term(chunk, lane, slot, level, level).wait_recv()
+                    total = hr[chunk, lane, slot].astype(F32)
+                    put(chunk, total, True)
+    else:
+        for chunk in range(CHUNKS):
+            prepare(chunk)
+            if span != out_rows:
+                @pl.loop(0, hp.shape[1] // span)
+                def _(group):
+                    column = pl.multiple_of(group * span, span)
+                    hp[chunk, pl.ds(column, span)] = partial(chunk, group).astype(BF16)
+
+            @pl.loop(0, levels - 1)
+            def _(number):
+                target = other_level(number)
+                if span == out_rows:
+                    hp[chunk, pl.ds(rows_of(target), out_rows)] = partial(chunk, target).astype(BF16)
+                term(chunk, 0, level, target, target).start()
+
             if span == out_rows:
-                fill(chunk, target)
-            term(chunk, target, level).start()
-
-        if span == out_rows:
-            fill(chunk, level)
-
-    mine = pl.ds(pl.multiple_of((2 * level + side) * out_rows, out_rows), out_rows)
-    for chunk in range(CHUNKS):
-        def add(number, total):
-            sender = other_level(number)
-            term(chunk, level, sender).wait_recv()
-            return total + hr[chunk, sender].astype(F32)
-
-        total = lax.fori_loop(0, levels - 1, add, hp[chunk, mine].astype(F32))
-        out_ref[0, :, chunk * wide : (chunk + 1) * wide] = total[:, :wide]
-        out_ref[1, :, chunk * wide : (chunk + 1) * wide] = total[:, wide:]
+                hp[chunk, pl.ds(rows_of(level), out_rows)] = partial(chunk, level).astype(BF16)
+
+        for chunk in range(CHUNKS):
+            def add(number, total):
+                sender = other_level(number)
+                term(chunk, 0, sender, level, sender).wait_recv()
+                return total + hr[chunk, 0, sender].astype(F32)
+
+            put(chunk, lax.fori_loop(0, levels - 1, add, hp[chunk, pl.ds(rows_of(level), out_rows)].astype(F32)))
 
     for number in range(len(ROUTES)):
         for index in range(PIECES):
@@ -289,33 +408,34 @@
 
         @pl.loop(0, levels - 1)
         def _(number):
-            term(chunk, other_level(number), level).wait_send()
+            target = other_level(number)
+            term(chunk, 0, target, target, target).wait_send()
+
+        if short_line(out_rows, levels) and levels > 3:
+            @pl.when((level == 2) | (levels - 1 - level == 2))
+            def _(chunk=chunk):
+                onward(chunk, 0, 0).wait_send()
 
 
 def shards(count_tile, green, direction, partners, counts):
     tile_dev, kmax = partners.shape
     rows, half = green.shape[1:]
-    tile = rows // tile_dev
     sources = direction.shape[2]
     out_rows = sources // count_tile
     levels = count_tile // 2
     wide = half // CHUNKS
-    me = lax.axis_index("tile")
-    step = 1 - 2 * (me % 2)
-    offsets = jnp.array(OFFSETS, jnp.int32) * step
-    block_tiles = (me + offsets)[:, None] * tile_dev + jnp.arange(tile_dev, dtype=jnp.int32)[None, :]
-    live = jnp.arange(kmax, dtype=jnp.int32)[None, :] < counts[:, None]
-    hit = (partners[None, :, None, :] == block_tiles[:, None, :, None]) & live[None, :, None, :]
-    mask = jnp.repeat(jnp.any(hit, axis=3).astype(F32), tile, axis=2)[:, :, None, :]
+    lanes = 2 if short_line(out_rows, levels) else 1
     anywhere = pl.BlockSpec(memory_space=pl.ANY)
     local = pl.BlockSpec(memory_space=pltpu.VMEM)
     dma = pltpu.SemaphoreType.DMA
     out = pl.pallas_call(
         functools.partial(kernel, count_tile),
-        out_shape=jax.ShapeDtypeStruct((2, out_rows, half), F32),
-        in_specs=[anywhere, anywhere, local],
+        out_shape=jax.ShapeDtypeStruct((out_rows, half // 64, 128), F32),
+        in_specs=[anywhere] * 4,
         out_specs=local,
         scratch_shapes=[
+            pltpu.SMEM((tile_dev, kmax), jnp.int32),
+            pltpu.SMEM((tile_dev,), jnp.int32),
             pltpu.VMEM((9, 2, rows, half), BF16),
             pltpu.VMEM((2, 2, half, half), BF16),
             pltpu.VMEM((2 * rows, half), BF16),
@@ -325,10 +445,11 @@
             pltpu.VMEM((FAR + 1, 2, rows, rows), F32),
             pltpu.VMEM((2 * rows, half), F32),
             pltpu.VMEM((CHUNKS, 2, 2 * rows, wide), BF16),
-            pltpu.VMEM((2, 2 * rows, 2 * wide), BF16),
+            pltpu.VMEM((levels if out_rows >= 128 else sources // 128, max(out_rows, 128), 4 * rows), BF16),
+            pltpu.VMEM((CHUNKS, 4 * rows, 2 * wide), BF16),
             pltpu.VMEM((CHUNKS, sources, 2 * wide), BF16),
-            pltpu.VMEM((CHUNKS, levels, out_rows, 2 * wide), BF16),
-            dma((3,)),
+            pltpu.VMEM((CHUNKS, lanes, levels + 1, out_rows, 2 * wide), BF16),
+            dma((5,)),
             dma((2,)),
             dma((len(ROUTES), PIECES)),
             dma((len(ROUTES), PIECES)),
@@ -339,13 +460,15 @@
             dma((CHUNKS,)),
             dma((CHUNKS,)),
             dma((CHUNKS, levels)),
-            dma((CHUNKS, levels)),
+            dma((CHUNKS, lanes, levels + 1)),
+            dma((CHUNKS,)),
         ],
         compiler_params=pltpu.CompilerParams(
             collective_id=0, has_side_effects=True, vmem_limit_bytes=56 * 1024 * 1024
         ),
-    )(green, direction, mask)
-    return jnp.swapaxes(out, 0, 1)
+    )(green, direction, partners, counts)
+    out = out.reshape(out_rows, half // 128, 2, 128)
+    return jnp.swapaxes(out, 1, 2).reshape(out_rows, 2, half)
 
 
 def solution(mesh):

time: 76.5 us -> 66.7 us (0.87)
  the two profiles are of different devices: /device:TPU:11 before, /device:TPU:0 now
where the time goes in v2:
time: 66.7 us; the launch traced here: 66.6 us
  Pallas kernels  64.7 us (97%)
  local copies, waits for them, and re-layouts  1.87 us (3%)
    pallas_call x1, Pallas kernels, shards(): pl.pallas_call(functools.partial(kernel, count_tile), out_shape=jax.Shape...  64.7 us
    unnamed x1, local copies, waits for them, and re-layouts  1.87 us

profile of v2, /device:TPU:0, one launch (start us, length us, event | category | flops | bytes accessed | tf_op | source)
XLA Modules:
  0.0 66.6 jit_solution(1231094794342886593)
XLA Ops:
  0.0 64.7 %shard_map.46 = f32[128,8,128]{2,1,0:T(8,128)} custom-call(bf16[2,256,512]{2,1,0:T(8,128)(2,1)} %a_ref.1, bf16[2,512,1024]{2,1,0:T(8,128)(2,1)} %v_ref.1, s32[2,8]{1,0:T(2,128)} %partners_ref.1, s32[2]{0:T(128)} %counts_ref.1), custom_call_target="tpu_custom_call" | custom-call | tf_op jit(solution)/shard_map/pallas_call | solution.py:431
  64.7 1.9 %copy.7 = f32[128,2,512]{2,1,0:T(2,128)} copy(f32[128,2,512]{2,1,0:T(2,128)} %bitcast.5) | data formatting | bytes 1048576

commit v3 on v2

--- a/solution.py
+++ b/solution.py
@@ -8,7 +8,7 @@
 from jax.sharding import PartitionSpec as P
 
 BAND_DEV = 3
-PIECES = 4
+PIECES = 8
 CHUNKS = 4
 OWN, ACROSS, NEAR, BACK, BACK_ACROSS, NEAR_ACROSS, FAR, PAIR, PAIR_ACROSS = range(9)
 OFFSETS = (0, 1, 2, -2, -1, 3, -3)
@@ -248,13 +248,15 @@
             job()
         arrive(4, index)
         send_route(5, index)
+    couple(BACK_ACROSS, NEAR_ACROSS)
     for index in range(PIECES):
         arrive(3, index)
-    couple(BACK_ACROSS, FAR)
+    couple(NEAR_ACROSS, FAR)
+    weigh(BACK_ACROSS, NEAR_ACROSS)
     for index in range(PIECES):
         arrive(5, index)
     couple(FAR, FAR + 1)
-    weigh(BACK_ACROSS, FAR + 1)
+    weigh(NEAR_ACROSS, FAR + 1)
 
     def w_copy(chunk):
         return remote(w.at[chunk, 0], w.at[chunk, 1], w_send.at[chunk], w_recv.at[chunk], across)
@@ -269,8 +271,9 @@
         return pl.multiple_of((2 * target + side) * out_rows, out_rows)
 
     def prepare(chunk):
-        w_copy(chunk).wait_recv()
         for block in range(2):
+            if block:
+                w_copy(chunk).wait_recv()
             top, low = w[chunk, block, :rows], w[chunk, block, rows:]
             first = 2 * rows * block
             rr[chunk, first : first + rows] = jnp.concatenate([top, low], axis=1)

time: 66.7 us -> 66.4 us (level)
  no operation moved by 1% of the time
where the time goes in v3:
time: 66.4 us; the launch traced here: 66.2 us
  Pallas kernels  64.3 us (97%)
  local copies, waits for them, and re-layouts  1.87 us (3%)
    pallas_call x1, Pallas kernels, shards(): pl.pallas_call(functools.partial(kernel, count_tile), out_shape=jax.Shape...  64.3 us
    unnamed x1, local copies, waits for them, and re-layouts  1.87 us

profile of v3, /device:TPU:0, one launch (start us, length us, event | category | flops | bytes accessed | tf_op | source)
XLA Modules:
  0.0 66.2 jit_solution(16873731078140879146)
XLA Ops:
  0.0 64.3 %shard_map.46 = f32[128,8,128]{2,1,0:T(8,128)} custom-call(bf16[2,256,512]{2,1,0:T(8,128)(2,1)} %a_ref.1, bf16[2,512,1024]{2,1,0:T(8,128)(2,1)} %v_ref.1, s32[2,8]{1,0:T(2,128)} %partners_ref.1, s32[2]{0:T(128)} %counts_ref.1), custom_call_target="tpu_custom_call" | custom-call | tf_op jit(solution)/shard_map/pallas_call | solution.py:434
  64.3 1.9 %copy.7 = f32[128,2,512]{2,1,0:T(2,128)} copy(f32[128,2,512]{2,1,0:T(2,128)} %bitcast.5) | data formatting | bytes 1048576
